TPU v7x, 256 devices: a whole 4x4x8 slice. The times are simulated.
256 devices in a mesh: dp: 32 (over x, y, z_lo), cent: 8 (over z_hi, core).
Axes of the slice: x: 4, y: 4, z: 8 (z_hi: 4, z_lo: 2; z = z_hi * 2 + z_lo), core: 2. Of those that a mesh axis runs over, the one named last changes fastest.
Arguments:
- points: bfloat16 [32768, 256], P('dp'), may hold values from -8 to 8
- centroids: bfloat16 [32768, 256], P('cent'), may hold values from -0.5 to 0.5
Outputs:
- new_centroids: float32 [32768, 256], P('cent')
- counts: float32 [32768], P('cent')
- log_evidence: float32 [32768], P('dp')
All inputs are finite; a program needn't handle non-finite values.
Results may differ from a plain program's by a relative error of at most 0.0016.
Values sent between devices are 32-bit elements; how exact they have to be, the bound alone decides.
A program may use at most 64 MiB of HBM per device.

v0:
```python
import math
import jax
import jax.numpy as jnp
from jax import lax
from jax.sharding import PartitionSpec as P

prior_mass = 0.5


def body(points, centroids):
    rows = points.shape[0]
    local_cent = centroids.shape[0]
    width = centroids.shape[1]
    every_centroid = local_cent * lax.axis_size("cent")
    block = min(512, rows)
    cnorm = jnp.einsum("kd,kd->k", centroids, centroids, preferred_element_type=jnp.float32)
    sums = jnp.zeros((local_cent, width), jnp.float32)
    counts = jnp.zeros((local_cent,), jnp.float32)
    evidence = []
    for step in range(rows // block):
        piece = lax.slice_in_dim(points, step * block, (step + 1) * block, axis=0)
        dots = jnp.einsum("nd,kd->nk", piece, centroids, preferred_element_type=jnp.float32)
        score = 2.0 * dots - cnorm[None, :]
        top = lax.pmax(jnp.max(score, axis=1), "cent")
        weights = jnp.exp(score - top[:, None])
        total = lax.psum(jnp.sum(weights, axis=1), "cent")
        resp = (weights / total[:, None]).astype(jnp.bfloat16)
        sums = sums + jnp.einsum("nk,nd->kd", resp, piece, preferred_element_type=jnp.float32)
        counts = counts + jnp.sum(resp.astype(jnp.float32), axis=0)
        evidence.append(top + jnp.log(total) - math.log(every_centroid))
    log_evidence = jnp.concatenate(evidence, axis=0)
    all_sums, all_counts = lax.psum((sums, counts), "dp")
    new_centroids = (all_sums + prior_mass * centroids.astype(jnp.float32)) / (
        all_counts + prior_mass
    )[:, None]
    return (new_centroids, all_counts, log_evidence)


def solution(mesh):
    return jax.shard_map(
        body,
        mesh=mesh,
        in_specs=(P("dp", None), P("cent", None)),
        out_specs=(P("cent", None), P("cent"), P("dp")),
        check_vma=False,
    )
```

profile of v0, /device:TPU:64, one launch (start us, length us, event | category | flops | bytes accessed | tf_op | source)
XLA Modules:
  0.0 424.3 jit_solution(17040239577599494853)
XLA Ops:
  7.2 0.0 copy-start.1
  7.2 0.0 copy-start.2
  7.2 0.0 all-reduce.4.cloned.1.call-start
  7.2 2.4 fusion.4
  9.6 3.0 fusion.12
  12.6 0.0 copy-done.1
  12.6 0.0 copy-done.2
  12.6 0.0 copy-start
  12.6 4.9 %fusion.1 = (f32[512]{0:T(512)S(1)}, f32[512]{0:T(512)S(1)}, f32[512,4096]{1,0:T(8,128)}) fusion(f32[4096]{0:T(1024)S(1)} %fusion.4, f32[512,4096]{1,0:T(8,128)S(1)} %fusion.12, bf16[4096,256]{1,0:T(8,128)(2,1)S(1)} %copy-done.1, bf16[1024,256]{1,0:T(8,128)(2,1)S(1)} %copy-done.2), kind=kOutput, calls=%fused_computation.9 | convolution fusion | flops 1086323712 | bytes 19156992 | tf_op jit(solution)/shard_map/nd,kd->nk/dot_general | solution.py:22
  17.6 0.8 copy-done
  18.3 15.2 %all-reduce.1 = (f32[512]{0:T(512)S(1)}, f32[512]{0:T(512)S(1)}) all-reduce(f32[512]{0:T(512)S(1)} %get-tuple-element.5, f32[512]{0:T(512)S(1)} %get-tuple-element.6), channel_id=1, replica_groups=mesh['dp'=32,'cent'=8] {'cent'}, use_global_device_ids=true, to_apply=%region_5.0 | all-reduce | flops 1024 | bytes 8192 | tf_op jit(solution)/shard_map/pmax | solution.py:24
  33.5 7.6 %fusion.3 = (f32[512]{0:T(512)S(1)}, f32[512]{0:T(512)S(1)}) fusion(f32[512,4096]{1,0:T(8,128)} %get-tuple-element.17, f32[512]{0:T(512)S(1)} %get-tuple-element.9, f32[4096]{0:T(1024)S(1)} %fusion.4, f32[512]{0:T(512)S(1)} %get-tuple-element.10, f32[512,4096]{1,0:T(8,128)} %copy-done), kind=kLoop, calls=%fused_computation.11 | loop fusion | flops 16776192 | bytes 16801792 | tf_op jit(solution)/shard_map/reduce_sum | solution.py:26
  41.2 14.2 %all-reduce = (f32[512]{0:T(512)S(1)}, f32[512]{0:T(512)S(1)}) all-reduce(f32[512]{0:T(512)S(1)} %get-tuple-element.4, f32[512]{0:T(512)S(1)} %get-tuple-element.3), channel_id=1, replica_groups=mesh['dp'=32,'cent'=8] {'cent'}, use_global_device_ids=true, to_apply=%region_3.0 | all-reduce | flops 1024 | bytes 8192 | tf_op jit(solution)/shard_map/psum | solution.py:26
  55.4 8.7 %convert_reduce_fusion = (f32[4096]{0:T(1024)S(1)}, bf16[512,4096]{1,0:T(8,128)(2,1)S(1)}, f32[4096]{0:T(1024)S(1)}, bf16[512,4096]{1,0:T(8,128)(2,1)S(1)}) fusion(f32[512]{0:T(512)S(1)} %get-tuple-element.8, f32[512]{0:T(512)S(1)} %get-tuple-element.9, f32[4096]{0:T(1024)S(1)} %fusion.4, f32[512,4096]{1,0:T(8,128)} %get-tuple-element.17, ...), kind=kLoop, calls=%fused_computation | loop fusion | flops 29351936 | bytes 25223168 | tf_op jit(solution)/shard_map/reduce_sum | solution.py:29
  64.0 1.3 fusion.10
  65.3 3.4 convolution_add_fusion
  68.7 0.0 all-reduce.4.cloned.1.call-update
  68.8 159.1 %psum.31 = f32[4096]{0:T(1024)S(1)} all-reduce(f32[4096]{0:T(1024)S(1)} %add.33), channel_id=1, replica_groups=mesh['dp'=32,'cent'=8] {'dp'}, use_global_device_ids=true, to_apply=%region_11.0 | all-reduce | flops 4096 | bytes 32768 | tf_op jit(solution)/shard_map/psum | solution.py:32
  227.8 0.0 copy-start.3
  227.9 0.6 pad_maximum_fusion
  228.5 185.1 %all-reduce.4.cloned.1.call-done = f32[4096,256]{1,0:T(8,128)} async-done(((f32[4096,256]{1,0:T(8,128)}), f32[4096,256]{1,0:T(8,128)}) %all-reduce.4.cloned.1.call-update) | async-done | bytes 4194320 | tf_op jit(solution)/shard_map/psum | solution.py:32
  413.5 3.9 fusion.6
  417.5 0.0 copy-done.3
  (3 shorter events, 0.0 us)
Async XLA Ops:
  7.2 5.4 %copy-start.1 = (bf16[4096,256]{1,0:T(8,128)(2,1)S(1)}, bf16[4096,256]{1,0:T(8,128)(2,1)}, u32[]{:S(2)}) copy-start(bf16[4096,256]{1,0:T(8,128)(2,1)} %param.3) | copy-start | bytes 6291460
  7.2 5.4 %copy-start.2 = (bf16[1024,256]{1,0:T(8,128)(2,1)S(1)}, bf16[1024,256]{1,0:T(8,128)(2,1)}, u32[]{:S(2)}) copy-start(bf16[1024,256]{1,0:T(8,128)(2,1)} %param.2) | copy-start | bytes 1572868
  7.2 406.4 %all-reduce.4.cloned.1.call-start = ((), (), s32[]{:S(2)}) async-start(), calls=%async_computation | async-start | bytes 8388608 | tf_op jit(solution)/shard_map/psum | solution.py:32
  12.6 5.7 %copy-start = (f32[512,4096]{1,0:T(8,128)}, f32[512,4096]{1,0:T(8,128)S(1)}, u32[]{:S(2)}) copy-start(f32[512,4096]{1,0:T(8,128)S(1)} %fusion.12) | copy-start | bytes 25165828
  227.8 189.7 %copy-start.3 = (f32[4096]{0:T(1024)}, f32[4096]{0:T(1024)S(1)}, u32[]{:S(2)}) copy-start(f32[4096]{0:T(1024)S(1)} %psum.31) | copy-start | bytes 49156
Sparse Core Ops, SparseCore 0:
  68.9 344.6 all-reduce.3
where the time goes:
time: 425 us; the launch traced here: 424 us
  blocking collectives  188 us (44%)
  waiting for transfers between devices  185 us (44%)
  other arithmetic  23.2 us (5%)
  between operations  14.1 us (3%)
  matrix products  12.6 us (3%)
    psum x1, waiting for transfers between devices, body(): all_sums, all_counts = lax.psum((sums, counts), 'dp')  185 us
    psum x1, blocking collectives, body(): all_sums, all_counts = lax.psum((sums, counts), 'dp')  159 us
    pmax x1, blocking collectives, body(): top = lax.pmax(jnp.max(score, axis=1), 'cent')  15.2 us
    psum x1, blocking collectives, body(): total = lax.psum(jnp.sum(weights, axis=1), 'cent')  14.2 us
    reduce_sum x1, other arithmetic, body(): counts = counts + jnp.sum(resp.astype(jnp.float32), axis=0)  8.66 us
  transfers between devices with their start and end apart: 1, of which 1 were waited for; matrix products, arithmetic and copies ran while one was open for 0% of the time, Pallas kernels for 0%

commit v1 on v0

--- a/solution.py
+++ b/solution.py
@@ -23,7 +23,7 @@
         score = 2.0 * dots - cnorm[None, :]
         top = lax.pmax(jnp.max(score, axis=1), "cent")
         weights = jnp.exp(score - top[:, None])
-        total = lax.psum(jnp.sum(weights, axis=1), "cent")
+        total = jnp.sum(lax.all_gather(jnp.sum(weights, axis=1), "cent"), axis=0)
         resp = (weights / total[:, None]).astype(jnp.bfloat16)
         sums = sums + jnp.einsum("nk,nd->kd", resp, piece, preferred_element_type=jnp.float32)
         counts = counts + jnp.sum(resp.astype(jnp.float32), axis=0)

time: 425 us -> 439 us (1.033)
  blocking collectives: 188 us -> 203 us
    all_gather x0 -> x2, blocking collectives: none -> 28.7 us  [body(): total = jnp.sum(lax.all_gather(jnp.sum(weights, axis=1), 'cent'), axis=0)]
    psum x1 -> x0, blocking collectives: 14.2 us -> none  [body(): total = lax.psum(jnp.sum(weights, axis=1), 'cent')]
where the time goes in v1:
time: 439 us
  blocking collectives  203 us (46%)
  waiting for transfers between devices  186 us (42%)
  other arithmetic  23.3 us (5%)
  between operations  14.1 us (3%)
  matrix products  12.6 us (3%)
    psum x1, waiting for transfers between devices, body(): all_sums, all_counts = lax.psum((sums, counts), 'dp')  186 us
    psum x1, blocking collectives, body(): all_sums, all_counts = lax.psum((sums, counts), 'dp')  159 us
    all_gather x2, blocking collectives, body(): total = jnp.sum(lax.all_gather(jnp.sum(weights, axis=1), 'cent'), axis=0)  28.7 us
    pmax x1, blocking collectives, body(): top = lax.pmax(jnp.max(score, axis=1), 'cent')  15.2 us
  transfers between devices with their start and end apart: 1, of which 1 were waited for; matrix products, arithmetic and copies ran while one was open for 0% of the time, Pallas kernels for 0%

profile of v1, /device:TPU:64, one launch (start us, length us, event | category | flops | bytes accessed | tf_op | source)
XLA Modules:
  0.0 439.1 jit_solution(15582138189369916906)
XLA Ops:
  7.2 0.0 copy-start.1
  7.2 0.0 copy-start.2
  7.2 0.0 all-reduce.3.cloned.1.call-start
  7.2 2.4 fusion.4
  9.6 3.0 fusion.12
  12.6 0.0 copy-done.1
  12.6 0.0 copy-done.2
  12.6 0.0 copy-start
  12.6 4.9 %fusion.1 = (f32[512]{0:T(512)S(1)}, f32[512]{0:T(512)S(1)}, f32[512,4096]{1,0:T(8,128)}) fusion(f32[4096]{0:T(1024)S(1)} %fusion.4, f32[512,4096]{1,0:T(8,128)S(1)} %fusion.12, bf16[4096,256]{1,0:T(8,128)(2,1)S(1)} %copy-done.1, bf16[1024,256]{1,0:T(8,128)(2,1)S(1)} %copy-done.2), kind=kOutput, calls=%fused_computation.9 | convolution fusion | flops 1086323712 | bytes 19156992 | tf_op jit(solution)/shard_map/nd,kd->nk/dot_general | solution.py:22
  17.6 0.8 copy-done
  18.3 15.2 %all-reduce = (f32[512]{0:T(512)S(1)}, f32[512]{0:T(512)S(1)}) all-reduce(f32[512]{0:T(512)S(1)} %get-tuple-element.5, f32[512]{0:T(512)S(1)} %get-tuple-element.6), channel_id=1, replica_groups=mesh['dp'=32,'cent'=8] {'cent'}, use_global_device_ids=true, to_apply=%region_5.0 | all-reduce | flops 1024 | bytes 8192 | tf_op jit(solution)/shard_map/pmax | solution.py:24
  33.5 7.6 %fusion.3 = (f32[512]{0:T(512)S(1)}, f32[512]{0:T(512)S(1)}) fusion(f32[512,4096]{1,0:T(8,128)} %get-tuple-element.15, f32[512]{0:T(512)S(1)} %get-tuple-element.7, f32[4096]{0:T(1024)S(1)} %fusion.4, f32[512]{0:T(512)S(1)} %get-tuple-element.8, f32[512,4096]{1,0:T(8,128)} %copy-done), kind=kLoop, calls=%fused_computation.11 | loop fusion | flops 16776192 | bytes 16801792 | tf_op jit(solution)/shard_map/reduce_sum | solution.py:26
  41.2 14.3 %all-gather.3 = f32[8,1,512]{2,1,0:T(1,128)S(1)} all-gather(f32[1,1,512]{2,1,0:T(1,128)S(1)} %bitcast.7), channel_id=3, replica_groups=mesh['dp'=32,'cent'=8] {'cent'}, dimensions={0}, use_global_device_ids=true | all-gather | bytes 18432 | tf_op jit(solution)/shard_map/all_gather | solution.py:26
  55.4 14.4 %all-gather.2 = f32[8,1,512]{2,1,0:T(1,128)S(1)} all-gather(f32[1,1,512]{2,1,0:T(1,128)S(1)} %bitcast.6), channel_id=2, replica_groups=mesh['dp'=32,'cent'=8] {'cent'}, dimensions={0}, use_global_device_ids=true | all-gather | bytes 18432 | tf_op jit(solution)/shard_map/all_gather | solution.py:26
  69.9 8.7 %convert_reduce_fusion = (f32[4096]{0:T(1024)S(1)}, bf16[512,4096]{1,0:T(8,128)(2,1)S(1)}, f32[4096]{0:T(1024)S(1)}, bf16[512,4096]{1,0:T(8,128)(2,1)S(1)}) fusion(f32[512]{0:T(512)S(1)} %reduce_sum.57, f32[512]{0:T(512)S(1)} %get-tuple-element.7, f32[4096]{0:T(1024)S(1)} %fusion.4, f32[512,4096]{1,0:T(8,128)} %get-tuple-element.15, f32[512]{0:T(512)S(1)} %reduce_sum.55, ...), kind=kLoop, calls=%fused_computation | loop fusion | flops 29351936 | bytes 25223168 | tf_op jit(solution)/shard_map/reduce_sum | solution.py:29
  78.6 1.3 fusion.10
  79.9 3.4 convolution_add_fusion
  83.3 0.0 all-reduce.3.cloned.1.call-update
  83.3 158.8 %psum.15 = f32[4096]{0:T(1024)S(1)} all-reduce(f32[4096]{0:T(1024)S(1)} %add.29), channel_id=1, replica_groups=mesh['dp'=32,'cent'=8] {'dp'}, use_global_device_ids=true, to_apply=%region_11.0 | all-reduce | flops 4096 | bytes 32768 | tf_op jit(solution)/shard_map/psum | solution.py:32
  242.1 0.0 copy-start.3
  242.1 0.6 pad_maximum_fusion
  242.7 185.6 %all-reduce.3.cloned.1.call-done = f32[4096,256]{1,0:T(8,128)} async-done(((f32[4096,256]{1,0:T(8,128)}), f32[4096,256]{1,0:T(8,128)}) %all-reduce.3.cloned.1.call-update) | async-done | bytes 4194320 | tf_op jit(solution)/shard_map/psum | solution.py:32
  428.3 3.9 fusion.6
  432.3 0.0 copy-done.3
  (6 shorter events, 0.1 us)
Async XLA Ops:
  7.2 5.4 %copy-start.1 = (bf16[4096,256]{1,0:T(8,128)(2,1)S(1)}, bf16[4096,256]{1,0:T(8,128)(2,1)}, u32[]{:S(2)}) copy-start(bf16[4096,256]{1,0:T(8,128)(2,1)} %param.3) | copy-start | bytes 6291460
  7.2 5.4 %copy-start.2 = (bf16[1024,256]{1,0:T(8,128)(2,1)S(1)}, bf16[1024,256]{1,0:T(8,128)(2,1)}, u32[]{:S(2)}) copy-start(bf16[1024,256]{1,0:T(8,128)(2,1)} %param.2) | copy-start | bytes 1572868
  7.2 421.2 %all-reduce.3.cloned.1.call-start = ((), (), s32[]{:S(2)}) async-start(), calls=%async_computation | async-start | bytes 8388608 | tf_op jit(solution)/shard_map/psum | solution.py:32
  12.6 5.7 %copy-start = (f32[512,4096]{1,0:T(8,128)}, f32[512,4096]{1,0:T(8,128)S(1)}, u32[]{:S(2)}) copy-start(f32[512,4096]{1,0:T(8,128)S(1)} %fusion.12) | copy-start | bytes 25165828
  242.1 190.2 %copy-start.3 = (f32[4096]{0:T(1024)}, f32[4096]{0:T(1024)S(1)}, u32[]{:S(2)}) copy-start(f32[4096]{0:T(1024)S(1)} %psum.15) | copy-start | bytes 49156
Sparse Core Ops, SparseCore 0:
  83.4 344.8 all-reduce.2
